TPU v7x, 512 devices: a whole 4x8x8 slice. The times are simulated.
512 devices in a mesh: ep: 64 (over z, x, core), tp: 8 (over y).
Axes of the slice: x: 4, y: 8, z: 8, core: 2. Of those that a mesh axis runs over, the one named last changes fastest.
Arguments:
- attn_out: bfloat16 [8192, 2048], P('ep', 'tp'), may hold values from -6 to 6
- resid: bfloat16 [8192, 2048], P(('ep', 'tp')), may hold values from -6 to 6
- norm_gain: float32 [2048], replicated, may hold values from 0.1 to 1.9
- expert_ids: int32 [8192, 6], P('ep'), may hold values from 0 to 63, all different within a row; in each aligned block of 128 rows (0 to 127, 128 to 255, ...) at most 16 rows name the same one
- gate_vals: float32 [8192, 6], P('ep'), may hold values from 0.1 to 1
- w_gate: bfloat16 [64, 1408, 2048], P('ep', 'tp'), may hold values from -0.125 to 0.125
- w_up: bfloat16 [64, 1408, 2048], P('ep', 'tp'), may hold values from -0.125 to 0.125
- w_down: bfloat16 [64, 1408, 2048], P('ep', 'tp'), may hold values from -0.15625 to 0.15625
Outputs:
- layer_out: bfloat16 [8192, 2048], P(('ep', 'tp'))
Inputs may be any that keep to these rules, and one draw needn't show every extreme that they name: `expert_ids`: among the tokens of one index of ep (aligned blocks of 128 rows), no expert is chosen by more than 16 tokens; some expert reaches 16 in some blocks. The experts of one token differ.
All inputs are finite; a program needn't handle non-finite values.
Results may differ from a plain program's by a relative error of at most 0.0095.
Values may be sent and summed in bfloat16 or wider, within the bound.
A program may use at most 64 MiB of HBM per device.

v0:
```python
import jax
import jax.numpy as jnp
from jax import lax
from jax.sharding import PartitionSpec as P

F32 = jnp.float32
BF16 = jnp.bfloat16


def per_device(attn_out, resid, norm_gain, expert_ids, gate_vals, w_gate, w_up, w_down):
    ep_count = lax.axis_size("ep")
    tok, top = expert_ids.shape
    cap = 4 * tok * top // (3 * ep_count)
    slots = ep_count * cap
    resid_cols = lax.all_to_all(resid, "tp", split_axis=1, concat_axis=0, tiled=True)
    down_cols = lax.all_to_all(w_down[0], "tp", split_axis=1, concat_axis=0, tiled=True)
    h = (resid_cols.astype(F32) + attn_out.astype(F32)).astype(BF16)
    hit = expert_ids[:, :, None] == jnp.arange(ep_count, dtype=jnp.int32)[None, None, :]
    chosen = jnp.any(hit, axis=1).astype(BF16)
    gates = jnp.sum(jnp.where(hit, gate_vals[:, :, None], 0.0), axis=1)
    earlier = jnp.tril(jnp.ones((tok, tok), BF16), -1)
    rank = jnp.dot(earlier, chosen, preferred_element_type=F32).astype(jnp.int32)
    place = (chosen[:, :, None] > 0) & (
        rank[:, :, None] == jnp.arange(cap, dtype=jnp.int32)[None, None, :]
    )
    weights = jnp.where(place, gates[:, :, None], 0.0).reshape(tok, slots)
    place = place.astype(BF16).reshape(tok, slots)
    send = lax.dot_general(place, h, (((0,), (0,)), ((), ())), preferred_element_type=F32).astype(
        BF16
    )
    got = lax.all_to_all(
        send.reshape(ep_count, cap, -1), "ep", split_axis=0, concat_axis=0, tiled=True
    )
    rows = lax.all_gather(got.reshape(slots, -1), "tp", axis=1, tiled=True)
    rows_f = rows.astype(F32)
    mean_sq = jnp.mean(rows_f * rows_f, axis=-1, keepdims=True)
    normed = (rows_f * lax.rsqrt(mean_sq + 1e-05) * norm_gain).astype(BF16)
    nt = (((1,), (1,)), ((), ()))
    gate_pre = lax.dot_general(w_gate[0], normed, nt, preferred_element_type=F32)
    up_pre = lax.dot_general(w_up[0], normed, nt, preferred_element_type=F32)
    act = (jax.nn.silu(gate_pre) * up_pre).astype(BF16)
    act_all = lax.all_gather(act, "tp", axis=0, tiled=True)
    out = lax.dot_general(
        act_all, down_cols, (((0,), (0,)), ((), ())), preferred_element_type=F32
    ).astype(BF16)
    back = lax.all_to_all(
        out.reshape(ep_count, cap, -1), "ep", split_axis=0, concat_axis=0, tiled=True
    )
    moe = jnp.dot(weights, back.reshape(slots, -1).astype(F32), precision=lax.Precision.HIGHEST)
    layer = (h.astype(F32) + moe).astype(BF16)
    return lax.all_to_all(layer, "tp", split_axis=0, concat_axis=1, tiled=True)


def solution(mesh):
    in_specs = (
        P("ep", "tp"),
        P(("ep", "tp"), None),
        P(),
        P("ep", None),
        P("ep", None),
        P("ep", "tp", None),
        P("ep", "tp", None),
        P("ep", "tp", None),
    )
    return jax.shard_map(
        per_device, mesh=mesh, in_specs=in_specs, out_specs=P(("ep", "tp"), None), check_vma=False
    )
```

profile of v0, /device:TPU:2, one launch (start us, length us, event | category | flops | bytes accessed | tf_op | source)
XLA Modules:
  0.0 219.9 jit_solution(954548781873976257)
XLA Ops:
  6.5 1.5 copy.37
  8.1 7.1 %all-to-all-start = ((bf16[16,8,256]{2,0,1:T(8,128)(2,1)}), bf16[16,8,256]{2,0,1:T(8,128)(2,1)S(1)}, u32[]{:S(2)}, u32[]{:S(2)}) async-start(bf16[16,8,256]{2,0,1:T(8,128)(2,1)} %bitcast.54), calls=%async_computation | async-start | bytes 131072 | tf_op jit(solution)/shard_map/all_to_all | solution.py:15
  15.2 0.7 fusion.19
  16.0 0.2 convolution_convert_fusion.2
  16.3 0.2 fusion.14
  16.5 7.1 %all-to-all-done = bf16[16,8,256]{2,0,1:T(8,128)(2,1)S(1)} async-done(((bf16[16,8,256]{2,0,1:T(8,128)(2,1)}), bf16[16,8,256]{2,0,1:T(8,128)(2,1)S(1)}, u32[]{:S(2)}, u32[]{:S(2)}) %all-to-all-start) | async-done | bytes 65568 | tf_op jit(solution)/shard_map/all_to_all | solution.py:15
  23.6 0.9 fusion.20
  24.4 0.3 convolution_convert_fusion.1
  24.7 31.3 %all_to_all.61 = bf16[64,16,256]{2,1,0:T(8,128)(2,1)} all-to-all(bf16[64,16,256]{2,1,0:T(8,128)(2,1)S(1)} %bitcast.57), channel_id=1, replica_groups=mesh['ep'=64,'tp'=8] {'ep'}, dimensions={0} | all-to-all | bytes 1048576 | tf_op jit(solution)/shard_map/all_to_all | solution.py:31
  56.1 56.3 %all-gather.3.cloned.1.call-done = bf16[1024,2048]{1,0:T(8,128)(2,1)} async-done(((bf16[1024,256]{1,0:T(8,128)(2,1)}), bf16[1024,2048]{1,0:T(8,128)(2,1)}) %all-gather.3.cloned.1.call-update) | async-done | bytes 4194320 | tf_op jit(solution)/shard_map/all_gather | solution.py:34
  112.4 3.2 %fusion = f32[1024]{0:T(1024)S(1)} fusion(bf16[1024,2048]{1,0:T(8,128)(2,1)} %all-gather.3.cloned.1.call-done), kind=kLoop, calls=%fused_computation.2 | loop fusion | flops 6290432 | bytes 4198400 | tf_op jit(solution)/shard_map/reduce_sum | solution.py:36
  115.7 0.2 copy-done.1
  115.9 1.7 convolution_bitcast_fusion.1
  117.5 2.6 %fusion.4 = bf16[176,1024]{1,0:T(8,128)(2,1)} fusion(bf16[1024,2048]{1,0:T(8,128)(2,1)S(1)} %copy-done.1, f32[2048]{0:T(1024)S(1)} %copy-done.6, f32[1024]{0:T(1024)S(1)} %add_rsqrt_fusion, bf16[1,176,2048]{2,1,0:T(8,128)(2,1)S(1)} %copy-done.5, f32[176,1024]{1,0:T(8,128)S(1)} %convolution_bitcast_fusion.1), kind=kOutput, calls=%fused_computation.10 | convolution fusion | flops 747667456 | bytes 6008832 | tf_op jit(solution)/shard_map/dot_general | solution.py:40
  120.1 0.2 copy.35
  120.3 0.1 copy.31
  120.5 23.5 %all_to_all.62 = bf16[176,8,256]{2,0,1:T(8,128)(2,1)S(1)} all-to-all(bf16[176,8,256]{2,0,1:T(8,128)(2,1)S(1)} %copy.31), channel_id=1, replica_groups=mesh['ep'=64,'tp'=8] {'tp'}, dimensions={1} | all-to-all | bytes 1441792 | tf_op jit(solution)/shard_map/all_to_all | solution.py:16
  144.0 23.3 %all-gather.5.cloned.1.call-done = bf16[1408,1024]{1,0:T(8,128)(2,1)} async-done(((bf16[176,1024]{1,0:T(8,128)(2,1)}), bf16[1408,1024]{1,0:T(8,128)(2,1)}) %all-gather.5.cloned.1.call-update) | async-done | bytes 2883600 | tf_op jit(solution)/shard_map/all_gather | solution.py:42
  167.3 3.6 %convolution_convert_fusion = bf16[1024,256]{1,0:T(8,128)(2,1)} fusion(bf16[1408,1024]{1,0:T(8,128)(2,1)} %all-gather.5.cloned.1.call-done, bf16[1408,256]{1,0:T(8,128)(2,1)S(1)} %bitcast.59), kind=kOutput, calls=%fused_computation.5 | convolution fusion | flops 738459648 | bytes 4128768 | tf_op jit(solution)/shard_map/dot_general | solution.py:43
  170.9 10.9 %all-to-all-start.3 = ((bf16[64,16,256]{2,1,0:T(8,128)(2,1)}), bf16[64,16,256]{2,1,0:T(8,128)(2,1)S(1)}, u32[]{:S(2)}, u32[]{:S(2)}) async-start(bf16[64,16,256]{2,1,0:T(8,128)(2,1)} %bitcast.12), calls=%async_computation.3 | async-start | bytes 1048576 | tf_op jit(solution)/shard_map/all_to_all | solution.py:46
  181.9 17.5 %all-to-all-done.3 = bf16[64,16,256]{2,1,0:T(8,128)(2,1)S(1)} async-done(((bf16[64,16,256]{2,1,0:T(8,128)(2,1)}), bf16[64,16,256]{2,1,0:T(8,128)(2,1)S(1)}, u32[]{:S(2)}, u32[]{:S(2)}) %all-to-all-start.3) | async-done | bytes 524320 | tf_op jit(solution)/shard_map/all_to_all | solution.py:46
  199.4 0.6 fusion.8
  200.0 12.5 %all_to_all.63 = bf16[8,16,256]{2,1,0:T(8,128)(2,1)S(1)} all-to-all(bf16[8,16,256]{2,1,0:T(8,128)(2,1)S(1)} %bitcast.62), channel_id=1, replica_groups=mesh['ep'=64,'tp'=8] {'tp'}, dimensions={0} | all-to-all | bytes 131072 | tf_op jit(solution)/shard_map/all_to_all | solution.py:51
  212.5 0.6 copy.34
  (23 shorter events, 0.3 us)
Async XLA Ops:
  6.5 109.1 %copy-start = (bf16[1,176,2048]{2,1,0:T(8,128)(2,1)S(1)}, bf16[1,176,2048]{2,1,0:T(8,128)(2,1)}, u32[]{:S(2)}) copy-start(bf16[1,176,2048]{2,1,0:T(8,128)(2,1)} %param.13) | copy-start | bytes 2162692
  6.5 109.1 %copy-start.6 = (f32[2048]{0:T(1024)S(1)}, f32[2048]{0:T(1024)}, u32[]{:S(2)}) copy-start(f32[2048]{0:T(1024)} %param.10) | copy-start | bytes 24580
  8.1 15.5 %all-to-all-start = ((bf16[16,8,256]{2,0,1:T(8,128)(2,1)}), bf16[16,8,256]{2,0,1:T(8,128)(2,1)S(1)}, u32[]{:S(2)}, u32[]{:S(2)}) async-start(bf16[16,8,256]{2,0,1:T(8,128)(2,1)} %bitcast.54), calls=%async_computation | async-start | bytes 131072 | tf_op jit(solution)/shard_map/all_to_all | solution.py:15
  15.2 97.2 %all-gather.3.cloned.1.call-start = ((), (), s32[]{:S(2)}) async-start(), calls=%async_computation.5 | async-start | bytes 4718592 | tf_op jit(solution)/shard_map/all_gather | solution.py:34
  56.1 111.2 %all-gather.5.cloned.1.call-start = ((), (), s32[]{:S(2)}) async-start(), calls=%async_computation.6 | async-start | bytes 3244032 | tf_op jit(solution)/shard_map/all_gather | solution.py:42
  112.4 3.4 %copy-start.1 = (bf16[1024,2048]{1,0:T(8,128)(2,1)S(1)}, bf16[1024,2048]{1,0:T(8,128)(2,1)}, u32[]{:S(2)}) copy-start(bf16[1024,2048]{1,0:T(8,128)(2,1)} %all-gather.3.cloned.1.call-done) | copy-start | bytes 12582916
  115.9 1.7 copy-start.5
  117.5 2.6 %copy-start.2 = (bf16[1,176,2048]{2,1,0:T(8,128)(2,1)S(1)}, bf16[1,176,2048]{2,1,0:T(8,128)(2,1)}, u32[]{:S(2)}) copy-start(bf16[1,176,2048]{2,1,0:T(8,128)(2,1)} %param.15) | copy-start | bytes 2162692
  120.5 61.3 %copy-start.3 = (s32[128,6]{0,1:T(8,128)S(1)}, s32[128,6]{0,1:T(8,128)}, u32[]{:S(2)}) copy-start(s32[128,6]{0,1:T(8,128)} %param.11) | copy-start | bytes 9220
  120.5 61.3 %copy-start.4 = (f32[128,6]{0,1:T(8,128)S(1)}, f32[128,6]{0,1:T(8,128)}, u32[]{:S(2)}) copy-start(f32[128,6]{0,1:T(8,128)} %param.12) | copy-start | bytes 9220
  170.9 28.4 %all-to-all-start.3 = ((bf16[64,16,256]{2,1,0:T(8,128)(2,1)}), bf16[64,16,256]{2,1,0:T(8,128)(2,1)S(1)}, u32[]{:S(2)}, u32[]{:S(2)}) async-start(bf16[64,16,256]{2,1,0:T(8,128)(2,1)} %bitcast.12), calls=%async_computation.3 | async-start | bytes 1048576 | tf_op jit(solution)/shard_map/all_to_all | solution.py:46
Sparse Core Ops, SparseCore 0:
  56.2 56.1 all-gather.2
  120.3 46.9 all-gather.4
where the time goes:
time: 220 us
  waiting for transfers between devices  104 us (47%)
  blocking collectives  67.3 us (31%)
  starting transfers between devices  18.1 us (8%)
  between operations  13.6 us (6%)
  matrix products  8.98 us (4%)
  other arithmetic  5.07 us (2%)
  local copies, waits for them, and re-layouts  2.79 us (1%)
    all_gather x1, waiting for transfers between devices, per_device(): rows = lax.all_gather(got.reshape(slots, -1), 'tp', axis=1, tiled=True)  56.3 us
    all_to_all x1, blocking collectives, per_device(): lax.all_to_all(send.reshape(ep_count, cap, -1), 'ep', split_axis=0, conca...  31.3 us
    all_to_all x1, blocking collectives, per_device(): lax.all_to_all(w_down[0], 'tp', split_axis=1, concat_axis=0, tiled=True)  23.5 us
    all_gather x1, waiting for transfers between devices, per_device(): act_all = lax.all_gather(act, 'tp', axis=0, tiled=True)  23.3 us
    all_to_all x1, waiting for transfers between devices, per_device(): lax.all_to_all(out.reshape(ep_count, cap, -1), 'ep', split_axis=0, concat...  17.5 us
    all_to_all x1, blocking collectives, per_device(): return lax.all_to_all(layer, 'tp', split_axis=0, concat_axis=1, tiled=True)  12.5 us
    all_to_all x1, starting transfers between devices, per_device(): lax.all_to_all(out.reshape(ep_count, cap, -1), 'ep', split_axis=0, concat...  10.9 us
    all_to_all x1, starting transfers between devices, per_device(): lax.all_to_all(resid, 'tp', split_axis=1, concat_axis=0, tiled=True)  7.1 us
  transfers between devices with their start and end apart: 4, of which 4 were waited for; matrix products, arithmetic and copies ran while one was open for 1% of the time, Pallas kernels for 0%

commit v1 on v0

--- a/solution.py
+++ b/solution.py
@@ -39,7 +39,9 @@
     gate_pre = lax.dot_general(w_gate[0], normed, nt, preferred_element_type=F32)
     up_pre = lax.dot_general(w_up[0], normed, nt, preferred_element_type=F32)
     act = (jax.nn.silu(gate_pre) * up_pre).astype(BF16)
-    act_all = lax.all_gather(act, "tp", axis=0, tiled=True)
+    act_all = jnp.concatenate(
+        lax.all_to_all(jnp.stack([act] * lax.axis_size("tp")), "tp", 0, 0), axis=0
+    )
     out = lax.dot_general(
         act_all, down_cols, (((0,), (0,)), ((), ())), preferred_element_type=F32
     ).astype(BF16)

time: 220 us -> 251 us (1.14)
  blocking collectives: 67.3 us -> 110 us
  waiting for transfers between devices: 104 us -> 90 us
  starting transfers between devices: 18.1 us -> 21.1 us
  matrix products: 8.98 us -> 6.29 us
    all_to_all x1, blocking collectives: 23.5 us -> 67.5 us  [per_device(): lax.all_to_all(jnp.stack([act] * lax.axis_size('tp')), 'tp', 0, 0)]
    all_gather x1 -> x0, waiting for transfers between devices: 23.3 us -> none  [per_device(): act_all = lax.all_gather(act, 'tp', axis=0, tiled=True)]
    all_gather x1, waiting for transfers between devices: 56.3 us -> 65.5 us  [per_device(): rows = lax.all_gather(got.reshape(slots, -1), 'tp', axis=1, tiled=True)]
    all_to_all x0 -> x1, starting transfers between devices: none -> 3.54 us  [per_device(): lax.all_to_all(w_down[0], 'tp', split_axis=1, concat_axis=0, tiled=True)]
  transfers between devices with their start and end apart: 4 -> 4, of which waited for: 4 -> 3; matrix products, arithmetic and copies ran while one was open for 1% -> 4% of each run, Pallas kernels for 0% -> 0%
where the time goes in v1:
time: 251 us
  blocking collectives  110 us (44%)
  waiting for transfers between devices  90 us (36%)
  starting transfers between devices  21.1 us (8%)
  between operations  13.6 us (5%)
  matrix products  6.29 us (3%)
  local copies, waits for them, and re-layouts  5.12 us (2%)
  other arithmetic  5.07 us (2%)
    all_to_all x1, blocking collectives, per_device(): lax.all_to_all(jnp.stack([act] * lax.axis_size('tp')), 'tp', 0, 0)  67.5 us
    all_gather x1, waiting for transfers between devices, per_device(): rows = lax.all_gather(got.reshape(slots, -1), 'tp', axis=1, tiled=True)  65.5 us
    all_to_all x1, blocking collectives, per_device(): lax.all_to_all(send.reshape(ep_count, cap, -1), 'ep', split_axis=0, conca...  31.3 us
    all_to_all x1, waiting for transfers between devices, per_device(): lax.all_to_all(out.reshape(ep_count, cap, -1), 'ep', split_axis=0, concat...  17.5 us
    all_to_all x1, blocking collectives, per_device(): return lax.all_to_all(layer, 'tp', split_axis=0, concat_axis=1, tiled=True)  10.8 us
    all_to_all x1, starting transfers between devices, per_device(): lax.all_to_all(out.reshape(ep_count, cap, -1), 'ep', split_axis=0, concat...  10.4 us
    all_to_all x1, starting transfers between devices, per_device(): lax.all_to_all(resid, 'tp', split_axis=1, concat_axis=0, tiled=True)  7.1 us
    all_to_all x1, waiting for transfers between devices, per_device(): lax.all_to_all(resid, 'tp', split_axis=1, concat_axis=0, tiled=True)  7.07 us
  transfers between devices with their start and end apart: 4, of which 3 were waited for; matrix products, arithmetic and copies ran while one was open for 4% of the time, Pallas kernels for 0%

profile of v1, /device:TPU:2, one launch (start us, length us, event | category | flops | bytes accessed | tf_op | source)
XLA Modules:
  0.0 250.7 jit_solution(17047149415699948302)
XLA Ops:
  6.5 1.5 copy.33
  8.1 7.1 %all-to-all-start = ((bf16[16,8,256]{2,0,1:T(8,128)(2,1)}), bf16[16,8,256]{2,0,1:T(8,128)(2,1)S(1)}, u32[]{:S(2)}, u32[]{:S(2)}) async-start(bf16[16,8,256]{2,0,1:T(8,128)(2,1)} %bitcast.57), calls=%async_computation | async-start | bytes 131072 | tf_op jit(solution)/shard_map/all_to_all | solution.py:15
  15.2 0.7 fusion.21
  16.0 0.2 convolution_convert_fusion.1
  16.3 0.2 fusion.16
  16.5 7.1 %all-to-all-done = bf16[16,8,256]{2,0,1:T(8,128)(2,1)S(1)} async-done(((bf16[16,8,256]{2,0,1:T(8,128)(2,1)}), bf16[16,8,256]{2,0,1:T(8,128)(2,1)S(1)}, u32[]{:S(2)}, u32[]{:S(2)}) %all-to-all-start) | async-done | bytes 65568 | tf_op jit(solution)/shard_map/all_to_all | solution.py:15
  23.6 0.9 fusion.22
  24.4 0.3 convolution_convert_fusion
  24.7 31.3 %all_to_all.63 = bf16[64,16,256]{2,1,0:T(8,128)(2,1)} all-to-all(bf16[64,16,256]{2,1,0:T(8,128)(2,1)S(1)} %bitcast.60), channel_id=1, replica_groups=mesh['ep'=64,'tp'=8] {'ep'}, dimensions={0} | all-to-all | bytes 1048576 | tf_op jit(solution)/shard_map/all_to_all | solution.py:31
  56.1 1.3 copy.31
  57.4 1.0 copy.27
  58.4 3.5 %all-to-all-start.3 = ((bf16[176,8,256]{2,0,1:T(8,128)(2,1)}), bf16[176,8,256]{2,0,1:T(8,128)(2,1)S(1)}, u32[]{:S(2)}, u32[]{:S(2)}) async-start(bf16[176,8,256]{2,0,1:T(8,128)(2,1)} %copy.27), calls=%async_computation.3 | async-start | bytes 1441792 | tf_op jit(solution)/shard_map/all_to_all | solution.py:16
  61.9 65.5 %all-gather.2.cloned.1.call-done = bf16[1024,2048]{1,0:T(8,128)(2,1)} async-done(((bf16[1024,256]{1,0:T(8,128)(2,1)}), bf16[1024,2048]{1,0:T(8,128)(2,1)}) %all-gather.2.cloned.1.call-update) | async-done | bytes 4194320 | tf_op jit(solution)/shard_map/all_gather | solution.py:34
  127.4 3.2 %fusion = f32[1024]{0:T(1024)S(1)} fusion(bf16[1024,2048]{1,0:T(8,128)(2,1)} %all-gather.2.cloned.1.call-done), kind=kLoop, calls=%fused_computation.2 | loop fusion | flops 6290432 | bytes 4198400 | tf_op jit(solution)/shard_map/reduce_sum | solution.py:36
  130.8 1.6 convolution_bitcast_fusion.2
  132.5 1.7 fusion.5
  134.2 0.4 stack.2
  134.6 67.5 %all_to_all.64 = bf16[8,176,1024]{2,1,0:T(8,128)(2,1)S(1)} all-to-all(bf16[8,176,1024]{2,1,0:T(8,128)(2,1)S(1)} %stack.2), channel_id=1, replica_groups=mesh['ep'=64,'tp'=8] {'tp'}, dimensions={0} | all-to-all | bytes 5767168 | tf_op jit(solution)/shard_map/all_to_all | solution.py:43
  202.1 1.8 fusion.3
  203.9 10.4 %all-to-all-start.4 = ((bf16[64,16,256]{2,1,0:T(8,128)(2,1)}), bf16[64,16,256]{2,1,0:T(8,128)(2,1)S(1)}, u32[]{:S(2)}, u32[]{:S(2)}) async-start(bf16[64,16,256]{2,1,0:T(8,128)(2,1)} %bitcast.12), calls=%async_computation.4 | async-start | bytes 1048576 | tf_op jit(solution)/shard_map/all_to_all | solution.py:48
  214.4 17.5 %all-to-all-done.4 = bf16[64,16,256]{2,1,0:T(8,128)(2,1)S(1)} async-done(((bf16[64,16,256]{2,1,0:T(8,128)(2,1)}), bf16[64,16,256]{2,1,0:T(8,128)(2,1)S(1)}, u32[]{:S(2)}, u32[]{:S(2)}) %all-to-all-start.4) | async-done | bytes 524320 | tf_op jit(solution)/shard_map/all_to_all | solution.py:48
  231.8 0.6 fusion.9
  232.4 10.8 %all_to_all.65 = bf16[8,16,256]{2,1,0:T(8,128)(2,1)S(1)} all-to-all(bf16[8,16,256]{2,1,0:T(8,128)(2,1)S(1)} %bitcast.64), channel_id=1, replica_groups=mesh['ep'=64,'tp'=8] {'tp'}, dimensions={0} | all-to-all | bytes 131072 | tf_op jit(solution)/shard_map/all_to_all | solution.py:53
  243.2 0.6 copy.30
  (21 shorter events, 0.4 us)
Async XLA Ops:
  6.5 124.1 %copy-start = (bf16[1,176,2048]{2,1,0:T(8,128)(2,1)S(1)}, bf16[1,176,2048]{2,1,0:T(8,128)(2,1)}, u32[]{:S(2)}) copy-start(bf16[1,176,2048]{2,1,0:T(8,128)(2,1)} %param.13) | copy-start | bytes 2162692
  8.1 15.5 %all-to-all-start = ((bf16[16,8,256]{2,0,1:T(8,128)(2,1)}), bf16[16,8,256]{2,0,1:T(8,128)(2,1)S(1)}, u32[]{:S(2)}, u32[]{:S(2)}) async-start(bf16[16,8,256]{2,0,1:T(8,128)(2,1)} %bitcast.57), calls=%async_computation | async-start | bytes 131072 | tf_op jit(solution)/shard_map/all_to_all | solution.py:15
  15.2 112.2 %all-gather.2.cloned.1.call-start = ((), (), s32[]{:S(2)}) async-start(), calls=%async_computation.6 | async-start | bytes 4718592 | tf_op jit(solution)/shard_map/all_gather | solution.py:34
  56.0 74.6 %copy-start.5 = (f32[2048]{0:T(1024)S(1)}, f32[2048]{0:T(1024)}, u32[]{:S(2)}) copy-start(f32[2048]{0:T(1024)} %param.10) | copy-start | bytes 24580
  58.4 75.8 %all-to-all-start.3 = ((bf16[176,8,256]{2,0,1:T(8,128)(2,1)}), bf16[176,8,256]{2,0,1:T(8,128)(2,1)S(1)}, u32[]{:S(2)}, u32[]{:S(2)}) async-start(bf16[176,8,256]{2,0,1:T(8,128)(2,1)} %copy.27), calls=%async_computation.3 | async-start | bytes 1441792 | tf_op jit(solution)/shard_map/all_to_all | solution.py:16
  127.4 3.4 %copy-start.1 = (bf16[1024,2048]{1,0:T(8,128)(2,1)S(1)}, bf16[1024,2048]{1,0:T(8,128)(2,1)}, u32[]{:S(2)}) copy-start(bf16[1024,2048]{1,0:T(8,128)(2,1)} %all-gather.2.cloned.1.call-done) | copy-start | bytes 12582916
  130.8 1.6 copy-start.4
  202.1 12.2 %copy-start.2 = (s32[128,6]{0,1:T(8,128)S(1)}, s32[128,6]{0,1:T(8,128)}, u32[]{:S(2)}) copy-start(s32[128,6]{0,1:T(8,128)} %param.11) | copy-start | bytes 9220
  202.1 12.2 %copy-start.3 = (f32[128,6]{0,1:T(8,128)S(1)}, f32[128,6]{0,1:T(8,128)}, u32[]{:S(2)}) copy-start(f32[128,6]{0,1:T(8,128)} %param.12) | copy-start | bytes 9220
  203.9 27.9 %all-to-all-start.4 = ((bf16[64,16,256]{2,1,0:T(8,128)(2,1)}), bf16[64,16,256]{2,1,0:T(8,128)(2,1)S(1)}, u32[]{:S(2)}, u32[]{:S(2)}) async-start(bf16[64,16,256]{2,1,0:T(8,128)(2,1)} %bitcast.12), calls=%async_computation.4 | async-start | bytes 1048576 | tf_op jit(solution)/shard_map/all_to_all | solution.py:48
Sparse Core Ops, SparseCore 0:
  56.2 71.1 all-gather.1
